TPU v7x, 32 devices: a whole 2x2x4 slice. The times are simulated.
32 devices in a mesh: seq: 4 (over y, x), ep: 8 (over z, core).
Axes of the slice: x: 2, y: 2, z: 4, core: 2. Of those that a mesh axis runs over, the one named last changes fastest.
Arguments:
- tokens: bfloat16 [24, 576, 768], P('ep', 'seq'), may hold values from -6 to 6
- routes: int32 [24, 576, 2], P('ep', 'seq'), may hold values from 0 to 31, all different within a row
- priority: int32 [24, 576], P('ep', 'seq'), may hold values from 0 to 431, as said below
- hires: int32 [8], P('ep'), may hold values from 0 to 3
- gain_one: float32 [768], replicated, may hold values from 0.1 to 1.9
- shift_one: float32 [768], replicated, may hold values from -1.8 to 1.8
- w_qkv: bfloat16 [768, 2304], replicated, may hold values from -0.21875 to 0.21875
- w_proj: bfloat16 [768, 768], replicated, may hold values from -6 to 6
- gain_two: float32 [768], replicated, may hold values from 0.1 to 1.9
- shift_two: float32 [768], replicated, may hold values from -1.8 to 1.8
- w_router: bfloat16 [768, 32], replicated, may hold values from -0.15917969 to 0.15917969
- expert_in: bfloat16 [98304, 768], P('ep'), may hold values from -0.21875 to 0.21875
- expert_out: bfloat16 [98304, 768], P('ep'), may hold values from -2.5 to 2.5
- cotangent: bfloat16 [24, 576, 768], P('ep', 'seq'), may hold values from -6 to 6
Outputs:
- output: bfloat16 [24, 576, 768], P('ep', 'seq')
- input_grad: bfloat16 [24, 576, 768], P('ep', 'seq')
- gain_one_grad: float32 [768], replicated
- shift_one_grad: float32 [768], replicated
- qkv_grad: float32 [768, 2304], replicated
- proj_grad: float32 [768, 768], replicated
- gain_two_grad: float32 [768], replicated
- shift_two_grad: float32 [768], replicated
- router_grad: float32 [768, 32], replicated
- expert_in_grad: float32 [98304, 768], P('ep')
- expert_out_grad: float32 [98304, 768], P('ep')
- rms_stats: float32 [3], replicated
Inputs may be any that keep to these rules, and one draw needn't show every extreme that they name: `priority`: within each device block of 3 images times 144 positions, the priorities are a permutation of 0 to 431.
All inputs are finite; a program needn't handle non-finite values.
Results may differ from a plain program's by a relative error of at most 0.015.
Values may be sent and summed in bfloat16 or wider, within the bound.
No kernel may reach another device: no remote copies, remote signals or barrier semaphores. Data moves between devices by JAX's collectives and lax.ppermute only.
A program may use at most 320 MiB of HBM per device.

v0:
```python
import jax
import jax.numpy as jnp
from jax import lax
from jax.sharding import PartitionSpec as P

HEADS = 12
EXPERTS = 32
TOP = 2
PATCHES = 576
SHORT = 196
norm_eps = 1e-06
neg_big = -1e30


def norm_forward(values, norm_gain, norm_bias):
    row_mean = jnp.mean(values, axis=-1, keepdims=True)
    centred = values - row_mean
    inv_root = lax.rsqrt(jnp.mean(centred * centred, axis=-1, keepdims=True) + norm_eps)
    normed = centred * inv_root
    return (normed * norm_gain + norm_bias, normed, inv_root)


def norm_backward(grad_out, normed, inv_root, norm_gain):
    gain_grad = jnp.sum(grad_out * normed, axis=0)
    bias_grad = jnp.sum(grad_out, axis=0)
    scaled = grad_out * norm_gain
    grad_in = inv_root * (
        scaled
        - jnp.mean(scaled, axis=-1, keepdims=True)
        - normed * jnp.mean(scaled * normed, axis=-1, keepdims=True)
    )
    return (grad_in, gain_grad, bias_grad)


def gelu_slope(values):
    return (
        0.5 * (1.0 + lax.erf(values * 0.7071067811865476))
        + values * jnp.exp(-0.5 * values * values) * 0.3989422804014327
    )


def routing(route_rows, priority_rows, row_valid, capacity):
    row_total = route_rows.shape[0]
    by_priority = (
        jnp.zeros((row_total,), jnp.int32)
        .at[priority_rows]
        .set(jnp.arange(row_total, dtype=jnp.int32))
    )
    ordered = jnp.concatenate([route_rows[by_priority, route_rank] for route_rank in range(TOP)])
    ordered_valid = jnp.concatenate([row_valid[by_priority]] * TOP)
    expert_hits = (
        ordered[:, None] == jnp.arange(EXPERTS, dtype=jnp.int32)[None, :]
    ) & ordered_valid[:, None]
    running = jnp.cumsum(expert_hits.astype(jnp.int32), axis=0)
    ordered_slot = jnp.sum(jnp.where(expert_hits, running, 0), axis=1) - 1
    pair_slot = ordered_slot.reshape(TOP, row_total)[:, priority_rows].T
    is_kept = (pair_slot >= 0) & (pair_slot < capacity)
    return jnp.where(is_kept, route_rows * capacity + pair_slot, EXPERTS * capacity)


def slot_sources(slot_dest, fill_value, capacity, divisor):
    flat_dest = slot_dest.reshape(-1)
    source_ids = jnp.arange(flat_dest.shape[0], dtype=jnp.int32) // divisor
    table_ids = (
        jnp.full((EXPERTS * capacity + 1,), fill_value, jnp.int32).at[flat_dest].set(source_ids)
    )
    return table_ids[: EXPERTS * capacity]


def fan_out(slot_table, ep_count, split_count, local_experts, capacity):
    feature_width = slot_table.shape[-1]
    grouped = slot_table.reshape(ep_count // split_count, 1, local_experts, capacity, feature_width)
    spread = jnp.broadcast_to(
        grouped, (ep_count // split_count, split_count, local_experts, capacity, feature_width)
    )
    return spread.reshape(ep_count, local_experts, capacity, feature_width)


def fan_in(arrived, split_count):
    ep_count, local_experts, capacity, feature_width = arrived.shape
    grouped = arrived.reshape(
        ep_count // split_count, split_count, local_experts, capacity, feature_width
    )
    return jnp.sum(grouped.astype(jnp.float32), axis=1).reshape(-1, feature_width)


def score_block(query_heads, key_heads, key_mask, score_scale):
    raw_scores = (
        jnp.einsum("ishd,ithd->ihst", query_heads, key_heads, preferred_element_type=jnp.float32)
        * score_scale
    )
    return jnp.where(key_mask[:, None, None, :], raw_scores, neg_big)


def per_device(
    tokens,
    routes,
    priority,
    hires,
    gain_one,
    shift_one,
    w_qkv,
    w_proj,
    gain_two,
    shift_two,
    w_router,
    expert_in,
    expert_out,
    cotangent,
):
    image_count, patch_rows, model_width = tokens.shape
    row_count = image_count * patch_rows
    seq_count = lax.axis_size("seq")
    ep_count = lax.axis_size("ep")
    full_patches = patch_rows * seq_count
    head_width = model_width // HEADS
    score_scale = head_width ** (-0.5)
    local_experts = max(1, EXPERTS // ep_count)
    split_count = max(1, ep_count // EXPERTS)
    local_hidden = expert_in.shape[0] // local_experts
    capacity = max(2, (105 * TOP * row_count + 100 * EXPERTS - 1) // (100 * EXPERTS))
    seq_place = lax.axis_index("seq")

    def send_slots(slot_table):
        outgoing = fan_out(slot_table, ep_count, split_count, local_experts, capacity)
        return lax.all_to_all(outgoing, "ep", split_axis=0, concat_axis=0, tiled=True)

    def return_slots(part_rows):
        returned = lax.all_to_all(part_rows, "ep", split_axis=0, concat_axis=0, tiled=True)
        return fan_in(returned, split_count)

    image_length = jnp.where(jnp.arange(image_count, dtype=jnp.int32) < hires[0], PATCHES, SHORT)
    key_mask = jnp.arange(full_patches, dtype=jnp.int32)[None, :] < image_length[:, None]
    own_mask = (seq_place * patch_rows + jnp.arange(patch_rows, dtype=jnp.int32))[
        None, :
    ] < image_length[:, None]
    row_valid = own_mask.reshape(row_count)
    valid_col = row_valid.astype(jnp.float32)[:, None]
    inputs = tokens.reshape(row_count, model_width).astype(jnp.float32)
    head_shape = (image_count, -1, HEADS, head_width)
    first_out, normed_one, inv_one = norm_forward(inputs, gain_one, shift_one)
    attn_in = first_out.astype(jnp.bfloat16)
    packed = jnp.dot(attn_in, w_qkv, preferred_element_type=jnp.float32).astype(jnp.bfloat16)
    query_rows = packed[:, :model_width].reshape(image_count, patch_rows, model_width)
    key_rows = packed[:, model_width : 2 * model_width].reshape(
        image_count, patch_rows, model_width
    )
    value_rows = packed[:, 2 * model_width :].reshape(image_count, patch_rows, model_width)
    query_heads = query_rows.reshape(head_shape)
    keys_all, values_all = (
        lax.all_gather(key_rows, "seq", axis=1, tiled=True),
        lax.all_gather(value_rows, "seq", axis=1, tiled=True),
    )
    scores = score_block(query_heads, keys_all.reshape(head_shape), key_mask, score_scale)
    row_max = jnp.max(scores, axis=-1, keepdims=True)
    exp_scores = jnp.exp(scores - row_max)
    row_total = jnp.sum(exp_scores, axis=-1, keepdims=True)
    probs = exp_scores / row_total
    log_total = row_max + jnp.log(row_total)
    attended = (
        jnp.einsum(
            "ihst,ithd->ishd",
            probs.astype(jnp.bfloat16),
            values_all.reshape(head_shape),
            preferred_element_type=jnp.float32,
        )
        .reshape(row_count, model_width)
        .astype(jnp.bfloat16)
    )
    attn_out = jnp.dot(attended, w_proj, preferred_element_type=jnp.float32)
    middle = inputs + attn_out
    second_out, normed_two, inv_two = norm_forward(middle, gain_two, shift_two)
    moe_in = second_out.astype(jnp.bfloat16)
    logits = jnp.dot(moe_in, w_router, preferred_element_type=jnp.float32)
    gate_probs = jax.nn.softmax(logits, axis=-1)
    route_rows = routes.reshape(row_count, TOP)
    slot_dest = routing(route_rows, priority.reshape(row_count), row_valid, capacity)
    token_src = slot_sources(slot_dest, row_count, capacity, TOP)
    pair_src = slot_sources(slot_dest, row_count * TOP, capacity, 1)
    padded_in = jnp.concatenate([moe_in, jnp.zeros((1, model_width), jnp.bfloat16)], axis=0)
    arrived = send_slots(padded_in[token_src])
    w_first = expert_in.reshape(local_experts, local_hidden, model_width)
    w_second = expert_out.reshape(local_experts, local_hidden, model_width)
    pre_act = jnp.einsum("secd,efd->secf", arrived, w_first, preferred_element_type=jnp.float32)
    hidden = jax.nn.gelu(pre_act, approximate=False).astype(jnp.bfloat16)
    partial_out = jnp.einsum(
        "secf,efd->secd", hidden, w_second, preferred_element_type=jnp.float32
    ).astype(jnp.bfloat16)
    value_table = return_slots(partial_out)
    padded_values = jnp.concatenate([value_table, jnp.zeros((1, model_width), jnp.float32)], axis=0)
    pair_values = padded_values[slot_dest.reshape(-1)].reshape(row_count, TOP, model_width)
    chosen = jnp.take_along_axis(gate_probs, route_rows, axis=1)
    moe_out = jnp.sum(chosen[:, :, None] * pair_values, axis=1)
    total = middle + moe_out
    output = (total * valid_col).astype(jnp.bfloat16).reshape(image_count, patch_rows, model_width)
    stat_terms = jnp.stack(
        [
            jnp.sum(valid_col * attn_out * attn_out),
            jnp.sum(valid_col * moe_out * moe_out),
            jnp.sum(valid_col * total * total),
            jnp.sum(row_valid.astype(jnp.float32)) * model_width,
        ]
    )
    grad_total = cotangent.reshape(row_count, model_width).astype(jnp.float32) * valid_col
    grad_gate = jnp.sum(grad_total[:, None, :] * pair_values, axis=2)
    grad_value = (
        (grad_total[:, None, :] * chosen[:, :, None])
        .astype(jnp.bfloat16)
        .reshape(row_count * TOP, model_width)
    )
    padded_grad = jnp.concatenate([grad_value, jnp.zeros((1, model_width), jnp.bfloat16)], axis=0)
    grad_sent = send_slots(padded_grad[pair_src])
    grad_hidden = jnp.einsum(
        "secd,efd->secf", grad_sent, w_second, preferred_element_type=jnp.float32
    )
    grad_pre = (grad_hidden * gelu_slope(pre_act)).astype(jnp.bfloat16)
    grad_second = jnp.einsum(
        "secf,secd->efd", hidden, grad_sent, preferred_element_type=jnp.float32
    ).reshape(-1, model_width)
    grad_first = jnp.einsum(
        "secf,secd->efd", grad_pre, arrived, preferred_element_type=jnp.float32
    ).reshape(-1, model_width)
    grad_part_in = jnp.einsum(
        "secf,efd->secd", grad_pre, w_first, preferred_element_type=jnp.float32
    ).astype(jnp.bfloat16)
    grad_in_table = return_slots(grad_part_in)
    padded_back = jnp.concatenate([grad_in_table, jnp.zeros((1, model_width), jnp.float32)], axis=0)
    grad_dispatch = jnp.sum(
        padded_back[slot_dest.reshape(-1)].reshape(row_count, TOP, model_width), axis=1
    )
    expert_ids = jnp.arange(EXPERTS, dtype=jnp.int32)
    grad_probs = jnp.sum(
        jnp.where(route_rows[:, :, None] == expert_ids[None, None, :], grad_gate[:, :, None], 0.0),
        axis=1,
    )
    grad_logits = (
        gate_probs * (grad_probs - jnp.sum(grad_probs * gate_probs, axis=-1, keepdims=True))
    ).astype(jnp.bfloat16)
    grad_router = jnp.einsum("rd,re->de", moe_in, grad_logits, preferred_element_type=jnp.float32)
    grad_moe_in = grad_dispatch + jnp.einsum(
        "re,de->rd", grad_logits, w_router, preferred_element_type=jnp.float32
    )
    grad_mid_norm, grad_gain_two, grad_shift_two = norm_backward(
        grad_moe_in, normed_two, inv_two, gain_two
    )
    grad_middle = grad_total + grad_mid_norm
    grad_attn = grad_middle.astype(jnp.bfloat16)
    grad_proj = jnp.einsum("rd,re->de", attended, grad_attn, preferred_element_type=jnp.float32)
    grad_attended = jnp.einsum(
        "re,de->rd", grad_attn, w_proj, preferred_element_type=jnp.float32
    ).astype(jnp.bfloat16)
    grad_heads = grad_attended.reshape(head_shape)
    keys_again, values_again = (
        lax.all_gather(key_rows, "seq", axis=1, tiled=True),
        lax.all_gather(value_rows, "seq", axis=1, tiled=True),
    )
    key_heads = keys_again.reshape(head_shape)
    value_heads = values_again.reshape(head_shape)
    probs_again = jnp.exp(score_block(query_heads, key_heads, key_mask, score_scale) - log_total)
    grad_probs_att = jnp.einsum(
        "ishd,ithd->ihst", grad_heads, value_heads, preferred_element_type=jnp.float32
    )
    delta = jnp.sum(grad_probs_att * probs_again, axis=-1, keepdims=True)
    grad_scores = (probs_again * (grad_probs_att - delta)).astype(jnp.bfloat16)
    grad_queries = (
        jnp.einsum("ihst,ithd->ishd", grad_scores, key_heads, preferred_element_type=jnp.float32)
        * score_scale
    )
    grad_keys_full = (
        jnp.einsum("ihst,ishd->ithd", grad_scores, query_heads, preferred_element_type=jnp.float32)
        * score_scale
    )
    grad_values_full = jnp.einsum(
        "ihst,ishd->ithd",
        probs_again.astype(jnp.bfloat16),
        grad_heads,
        preferred_element_type=jnp.float32,
    )
    grad_keys, grad_values = (
        lax.psum_scatter(
            grad_keys_full.reshape(image_count, full_patches, model_width),
            "seq",
            scatter_dimension=1,
            tiled=True,
        ),
        lax.psum_scatter(
            grad_values_full.reshape(image_count, full_patches, model_width),
            "seq",
            scatter_dimension=1,
            tiled=True,
        ),
    )
    grad_packed = jnp.concatenate(
        [
            grad_queries.reshape(row_count, model_width),
            grad_keys.reshape(row_count, model_width),
            grad_values.reshape(row_count, model_width),
        ],
        axis=1,
    ).astype(jnp.bfloat16)
    grad_qkv = jnp.einsum("rd,re->de", attn_in, grad_packed, preferred_element_type=jnp.float32)
    grad_attn_in = jnp.einsum("re,de->rd", grad_packed, w_qkv, preferred_element_type=jnp.float32)
    grad_in_norm, grad_gain_one, grad_shift_one = norm_backward(
        grad_attn_in, normed_one, inv_one, gain_one
    )
    input_grad = (
        (grad_middle + grad_in_norm)
        .astype(jnp.bfloat16)
        .reshape(image_count, patch_rows, model_width)
    )
    summed = lax.psum(
        (
            grad_qkv,
            grad_proj,
            grad_router,
            grad_gain_one,
            grad_shift_one,
            grad_gain_two,
            grad_shift_two,
            stat_terms,
        ),
        ("seq", "ep"),
    )
    expert_grads = (
        lax.psum(grad_first.astype(jnp.bfloat16), "seq").astype(jnp.float32),
        lax.psum(grad_second.astype(jnp.bfloat16), "seq").astype(jnp.float32),
    )
    rms_stats = jnp.sqrt(summed[7][:3] / summed[7][3])
    return (
        output,
        input_grad,
        summed[3],
        summed[4],
        summed[0],
        summed[1],
        summed[5],
        summed[6],
        summed[2],
        expert_grads[0],
        expert_grads[1],
        rms_stats,
    )


def solution(mesh):
    in_specs = (
        P("ep", "seq", None),
        P("ep", "seq", None),
        P("ep", "seq"),
        P("ep"),
        P(),
        P(),
        P(),
        P(),
        P(),
        P(),
        P(),
        P("ep", None),
        P("ep", None),
        P("ep", "seq", None),
    )
    out_specs = (
        P("ep", "seq", None),
        P("ep", "seq", None),
        P(),
        P(),
        P(),
        P(),
        P(),
        P(),
        P(),
        P("ep", None),
        P("ep", None),
        P(),
    )
    return jax.shard_map(
        per_device, mesh=mesh, in_specs=in_specs, out_specs=out_specs, check_vma=False
    )
```

profile of v0, /device:TPU:0, one launch (start us, length us, event | category | flops | bytes accessed | tf_op | source)
XLA Modules:
  0.0 1413.0 jit_solution(5902060563627623308)
XLA Ops:
  15.6 3.3 reshape_reshape.9
  18.9 3.8 copy.111
  28.5 6.5 gather_fusion
  35.0 7.7 gather_fusion.1
  44.1 4.0 gather_fusion.2
  50.4 4.8 reduce-window.6
  65.3 5.5 scatter_custom_fusion.1
  71.5 5.4 copy.110
  76.9 5.0 fusion.69
  81.9 5.0 copy-done.1
  86.9 3.8 fusion.23
  90.7 9.3 all-gather.3.cloned.1.call-done
  100.0 5.3 copy.109
  105.3 8.2 fusion.37
  113.5 4.0 copy.112
  117.5 3.5 convert_element_type.128
  121.0 3.5 fusion.67
  127.9 6.7 gather_fusion.4
  137.0 3.6 copy.119
  140.7 5.1 all-to-all-start
  156.2 4.6 mul.269
  160.8 5.4 scatter_custom_fusion.2
  169.5 12.0 gather_fusion.8
  184.7 7.0 gather_fusion.6
  194.2 3.7 copy.124
  197.8 5.3 all-to-all-start.2
  203.2 35.2 %fusion.2 = (bf16[8,4,29,3072]{3,2,0,1:T(8,128)(2,1)S(1)}, f32[4,8,29,3072]{3,2,1,0:T(8,128)}) fusion(bf16[4,3072,768,1]{2,1,3,0:T(8,128)(2,1)} %bitcast.184, bf16[8,4,29,768]{3,1,2,0:T(4,128)(2,1)} %all-to-all-done), kind=kOutput, calls=%fused_computation.24 | convolution fusion | flops 4564156416 | bytes 37404672 | tf_op jit(solution)/shard_map/secd,efd->secf/dot_general | solution.py:184
  238.3 11.5 fusion.30
  252.0 5.6 all-to-all-start.1
  257.6 13.6 fusion.8
  271.3 11.5 fusion.31
  285.0 7.3 all-to-all-done.1
  292.3 4.3 all-to-all-start.3
  310.3 6.7 gather_fusion.5
  317.0 4.4 reshape.414
  321.4 7.5 multiply_reduce_fusion.1
  342.1 6.7 gather_fusion.7
  348.8 4.6 reshape.418
  353.4 6.0 reduce_sum.241
  359.5 5.4 fusion.41
  368.1 3.3 reshape.419
  371.4 3.8 copy.130
  375.2 14.9 %multiply_reduce_fusion = (f32[3,12,144]{2,1,0:T(8,128)S(1)}, f32[3,12,144,576]{3,2,1,0:T(8,128)}) fusion(f32[3,12,144,576]{3,2,1,0:T(8,128)} %copy-done.1, f32[3,12,144]{2,1,0:T(8,128)} %log_add_fusion, bf16[3,144,12,64]{1,3,2,0:T(8,128)(2,1)} %copy.130, bf16[3,576,12,64]{1,3,2,0:T(8,128)(2,1)} %bitcast.170), kind=kOutput, calls=%fused_computation.17 | convolution fusion | flops 391158720 | bytes 27247104 | tf_op jit(solution)/shard_map/ishd,ithd->ihst/dot_general | solution.py:260
  390.1 9.9 multiply_convert_fusion
  400.1 4.2 broadcast_multiply_fusion
  404.7 7.5 copy.133
  412.2 9.9 fusion.25
  422.1 7.5 copy.135
  429.7 12.3 bitcast_convert_fusion
  442.0 12.1 bitcast_convert_fusion.1
  454.2 8.4 fusion.38
  462.6 4.2 copy.131
  466.9 3.5 reshape.420
  472.4 3.7 fusion.44
  478.4 61.2 %reduce-scatter.5.cloned.1.call-done = f32[3,144,768]{2,1,0:T(8,128)} async-done(((f32[3,576,768]{2,1,0:T(8,128)}), f32[3,144,768]{2,1,0:T(8,128)}) %reduce-scatter.5.cloned.1.call-update) | async-done | bytes 1327120 | tf_op jit(solution)/shard_map/reduce_scatter | solution.py:286
  541.8 6.5 fusion.42
  551.5 5.5 multiply_reduce_fusion.4
  557.0 40.4 %all-reduce.7 = (f32[768]{0:T(1024)}, f32[768]{0:T(1024)}, f32[768]{0:T(1024)}, f32[768]{0:T(1024)}, f32[4]{0:T(128)}) all-reduce(f32[768]{0:T(1024)} %get-tuple-element.17, f32[768]{0:T(1024)} %get-tuple-element.26, f32[768]{0:T(1024)S(1)} %copy-done.36, f32[768]{0:T(1024)S(1)} %copy-done.37, ...), channel_id=1, replica_groups=mesh['seq'=4,'ep'=8] {'seq','ep'}, use_global_device_ids=true, to_apply=%region_27.28 | all-reduce | flops 3076 | bytes 24608 | tf_op jit(solution)/shard_map/psum | solution.py:311
  605.1 588.1 %all-reduce.15.cloned.1.call-done = (bf16[12288,768]{1,0:T(8,128)(2,1)}, bf16[12288,768]{1,0:T(8,128)(2,1)}) async-done(((bf16[12288,768]{1,0:T(8,128)(2,1)}, bf16[12288,768]{1,0:T(8,128)(2,1)}), (bf16[12288,768]{1,0:T(8,128)(2,1)}, bf16[12288,768]{1,0:T(8,128)(2,1)})) %all-reduce.15.cloned.1.call-update) | async-done | bytes 37748752 | tf_op jit(solution)/shard_map/psum | solution.py:325
  1193.2 21.1 %convert_element_type.149 = f32[12288,768]{1,0:T(8,128)} convert(bf16[12288,768]{1,0:T(8,128)(2,1)} %get-tuple-element.36) | non-fusion elementwise | flops 9437184 | bytes 56623104 | tf_op jit(solution)/shard_map/convert_element_type | solution.py:325
  1214.2 4.6 copy-done.6
  1218.9 12.9 convert_element_type.152
  1231.8 165.5 %all-reduce.13.cloned.1.call-done = (f32[768,2304]{1,0:T(8,128)}, f32[768,768]{1,0:T(8,128)}, f32[768,32]{0,1:T(8,128)}) async-done(((f32[768,2304]{1,0:T(8,128)}, f32[768,768]{1,0:T(8,128)}, f32[768,32]{0,1:T(8,128)}), (f32[768,2304]{1,0:T(8,128)}, f32[768,768]{1,0:T(8,128)}, f32[768,32]{0,1:T(8,128)})) %all-reduce.13.cloned.1.call-update) | async-done | bytes 9535504 | tf_op jit(solution)/shard_map/psum | solution.py:311
  1397.3 6.6 copy.162
  (205 shorter events, 106.9 us)
Async XLA Ops:
  7.2 4.6 copy-start
  7.2 64.3 %all-gather.5.cloned.1.call-start = ((), (), s32[]{:S(2)}) async-start(), calls=%async_computation.7 | async-start | bytes 3317760 | tf_op jit(solution)/shard_map/all_gather | solution.py:151
  10.2 3.3 copy-start.32
  10.3 3.2 copy-start.34
  11.8 1.8 copy-start.12
  14.9 85.1 %all-gather.3.cloned.1.call-start = ((), (), s32[]{:S(2)}) async-start(), calls=%async_computation.6 | async-start | bytes 3317760 | tf_op jit(solution)/shard_map/all_gather | solution.py:152
  14.9 8.9 copy-start.31
  15.6 9.1 copy-start.44
  24.8 0.6 copy-start.41
  49.0 6.3 copy-start.43
  65.3 5.5 copy-start.39
  81.9 5.0 copy-start.1
  81.9 5.0 copy-start.17
  121.0 4.5 copy-start.23
  121.0 4.5 copy-start.42
  124.5 1.1 copy-start.3
  124.5 1.3 copy-start.19
  125.6 0.6 copy-start.27
  126.1 0.9 copy-start.8
  140.7 57.1 %all-to-all-start = ((bf16[8,4,29,768]{3,1,2,0:T(4,128)(2,1)}), bf16[8,4,29,768]{3,1,2,0:T(4,128)(2,1)}, u32[]{:S(2)}, u32[]{:S(2)}) async-start(bf16[8,4,29,768]{3,1,2,0:T(4,128)(2,1)} %copy.119), calls=%async_computation | async-start | bytes 2850816 | tf_op jit(solution)/shard_map/all_to_all | solution.py:126
  146.5 9.8 copy-start.25
  152.7 1.1 copy-start.7
  167.7 0.6 copy-start.15
  167.7 0.6 copy-start.21
  168.3 0.6 copy-start.29
  169.5 12.0 copy-start.38
  197.8 54.2 %all-to-all-start.2 = ((bf16[8,4,29,768]{3,1,2,0:T(4,128)(2,1)}), bf16[8,4,29,768]{3,1,2,0:T(4,128)(2,1)}, u32[]{:S(2)}, u32[]{:S(2)}) async-start(bf16[8,4,29,768]{3,1,2,0:T(4,128)(2,1)} %copy.124), calls=%async_computation.2 | async-start | bytes 2850816 | tf_op jit(solution)/shard_map/all_to_all | solution.py:126
  238.3 11.5 copy-start.46
  252.0 40.3 %all-to-all-start.1 = ((bf16[8,4,29,768]{3,1,2,0:T(4,128)(2,1)}), bf16[8,4,29,768]{3,1,2,0:T(4,128)(2,1)}, u32[]{:S(2)}, u32[]{:S(2)}) async-start(bf16[8,4,29,768]{3,1,2,0:T(4,128)(2,1)} %copy.121), calls=%async_computation.1 | async-start | bytes 2850816 | tf_op jit(solution)/shard_map/all_to_all | solution.py:129
  271.3 11.5 copy-start.45
  282.8 15.0 %copy-start.40 = (s32[864]{0:T(1024)S(1)}, s32[864]{0:T(1024)}, u32[]{:S(2)}) copy-start(s32[864]{0:T(1024)} %copy-done.39) | copy-start | bytes 10372
  292.3 41.4 %all-to-all-start.3 = ((bf16[8,4,29,768]{3,1,2,0:T(4,128)(2,1)}), bf16[8,4,29,768]{3,1,2,0:T(4,128)(2,1)}, u32[]{:S(2)}, u32[]{:S(2)}) async-start(bf16[8,4,29,768]{3,1,2,0:T(4,128)(2,1)} %copy.126), calls=%async_computation.3 | async-start | bytes 2850816 | tf_op jit(solution)/shard_map/all_to_all | solution.py:129
  296.6 179.5 %reduce-scatter.3.cloned.1.call-start = ((), (), s32[]{:S(2)}) async-start(), calls=%async_computation.8 | async-start | bytes 6635520 | tf_op jit(solution)/shard_map/reduce_scatter | solution.py:280
  321.4 9.9 copy-start.22
  321.4 9.9 copy-start.30
  353.4 6.0 copy-start.20
  353.4 6.0 copy-start.24
  353.4 6.0 copy-start.26
  353.4 6.0 copy-start.28
  359.4 5.5 copy-start.4
  359.4 5.4 copy-start.11
  364.9 1.7 copy-start.10
  365.4 1.1 copy-start.5
  375.2 14.9 %copy-start.16 = (f32[3,12,144]{2,1,0:T(8,128)S(1)}, f32[3,12,144]{2,1,0:T(8,128)}, u32[]{:S(2)}) copy-start(f32[3,12,144]{2,1,0:T(8,128)} %log_add_fusion) | copy-start | bytes 62212
  390.1 9.9 copy-start.9
  400.1 4.6 copy-start.2
  412.1 127.4 %reduce-scatter.5.cloned.1.call-start = ((), (), s32[]{:S(2)}) async-start(), calls=%async_computation.9 | async-start | bytes 6635520 | tf_op jit(solution)/shard_map/reduce_scatter | solution.py:286
  429.7 763.5 %all-reduce.15.cloned.1.call-start = ((), (), s32[]{:S(2)}) async-start(), calls=%async_computation.11 | async-start | bytes 75497472 | tf_op jit(solution)/shard_map/psum | solution.py:325
  454.2 943.1 %all-reduce.13.cloned.1.call-start = ((), (), s32[]{:S(2)}) async-start(), calls=%async_computation.10 | async-start | bytes 19070976 | tf_op jit(solution)/shard_map/psum | solution.py:311
  540.9 0.8 copy-start.13
  548.3 3.2 copy-start.33
  548.3 3.2 copy-start.35
  551.5 5.5 copy-start.36
  551.5 5.5 copy-start.37
  1193.2 25.7 %copy-start.6 = (bf16[12288,768]{1,0:T(8,128)(2,1)S(1)}, bf16[12288,768]{1,0:T(8,128)(2,1)}, u32[]{:S(2)}) copy-start(bf16[12288,768]{1,0:T(8,128)(2,1)} %get-tuple-element.37) | copy-start | bytes 56623108
  1397.3 6.6 copy-start.14
  1403.9 1.4 copy-start.18
Sparse Core Ops, SparseCore 0:
  15.0 42.6 all-gather.4
  60.1 39.9 all-gather.2
  412.3 62.3 reduce-scatter.2
  477.5 61.9 reduce-scatter.4
  543.7 649.4 all-reduce.14
  1201.5 195.7 all-reduce.12
where the time goes:
time: 1420 us; the launch traced here: 1410 us
  waiting for transfers between devices  832 us (59%)
  local copies, waits for them, and re-layouts  215 us (15%)
  matrix products  178 us (13%)
  other arithmetic  110 us (8%)
  blocking collectives  40.4 us (3%)
  starting transfers between devices  20.5 us (1%)
  between operations  16.3 us (1%)
    psum x1, waiting for transfers between devices, per_device(): lax.psum(grad_first.astype(jnp.bfloat16), 'seq').astype(jnp.float32)  588 us
    psum x1, waiting for transfers between devices, per_device(): lax.psum((grad_qkv, grad_proj, grad_router, grad_gain_one, grad_shift_one...  165 us
    reduce_scatter x1, waiting for transfers between devices, per_device(): lax.psum_scatter(grad_values_full.reshape(image_count, full_patches, mode...  61.2 us
    psum x1, blocking collectives, per_device(): lax.psum((grad_qkv, grad_proj, grad_router, grad_gain_one, grad_shift_one...  40.4 us
    dot_general x1, matrix products, per_device(): jnp.einsum('secd,efd->secf', arrived, w_first, preferred_element_type=jnp...  35.2 us
  transfers between devices with their start and end apart: 10, of which 5 were waited for; matrix products, arithmetic and copies ran while one was open for 25% of the time, Pallas kernels for 0%

commit v1 on v0

--- a/solution.py
+++ b/solution.py
@@ -308,7 +308,13 @@
         .astype(jnp.bfloat16)
         .reshape(image_count, patch_rows, model_width)
     )
-    summed = lax.psum(
+
+    def see_files_now(u):
+        for ii in ("ep", "seq"):
+            u = lax.psum(u, ii)
+        return u
+
+    summed = see_files_now(
         (
             grad_qkv,
             grad_proj,
@@ -318,8 +324,7 @@
             grad_gain_two,
             grad_shift_two,
             stat_terms,
-        ),
-        ("seq", "ep"),
+        )
     )
     expert_grads = (
         lax.psum(grad_first.astype(jnp.bfloat16), "seq").astype(jnp.float32),

time: 1420 us -> 1620 us (1.14)
  waiting for transfers between devices: 832 us -> 1030 us
    psum x1 -> x2, waiting for transfers between devices: 165 us -> 333 us  [see_files_now(): u = lax.psum(u, ii)]
    reduce_scatter x1, waiting for transfers between devices: 0.01 us -> 23.9 us  [per_device(): lax.psum_scatter(grad_keys_full.reshape(image_count, full_patches, model_...]
    psum x1 -> x2, blocking collectives: 40.4 us -> 47.2 us  [see_files_now(): u = lax.psum(u, ii)]
  transfers between devices with their start and end apart: 10 -> 11, of which waited for: 5 -> 7; matrix products, arithmetic and copies ran while one was open for 25% -> 21% of each run, Pallas kernels for 0% -> 0%
where the time goes in v1:
time: 1620 us; the launch traced here: 1610 us
  waiting for transfers between devices  1030 us (64%)
  local copies, waits for them, and re-layouts  215 us (13%)
  matrix products  178 us (11%)
  other arithmetic  110 us (7%)
  blocking collectives  47.2 us (3%)
  starting transfers between devices  20.5 us (1%)
  between operations  16.3 us (1%)
    psum x1, waiting for transfers between devices, per_device(): lax.psum(grad_first.astype(jnp.bfloat16), 'seq').astype(jnp.float32)  591 us
    psum x2, waiting for transfers between devices, see_files_now(): u = lax.psum(u, ii)  333 us
    reduce_scatter x1, waiting for transfers between devices, per_device(): lax.psum_scatter(grad_values_full.reshape(image_count, full_patches, mode...  63.2 us
    psum x2, blocking collectives, see_files_now(): u = lax.psum(u, ii)  47.2 us
    dot_general x1, matrix products, per_device(): jnp.einsum('secd,efd->secf', arrived, w_first, preferred_element_type=jnp...  35.2 us
  transfers between devices with their start and end apart: 11, of which 7 were waited for; matrix products, arithmetic and copies ran while one was open for 21% of the time, Pallas kernels for 0%

profile of v1, /device:TPU:0, one launch (start us, length us, event | category | flops | bytes accessed | tf_op | source)
XLA Modules:
  0.0 1614.5 jit_solution(942727287853634670)
XLA Ops:
  18.9 3.8 copy.111
  28.5 6.5 gather_fusion
  35.0 7.7 gather_fusion.1
  44.1 4.0 gather_fusion.2
  50.4 4.8 reduce-window.6
  65.3 5.5 scatter_custom_fusion.1
  71.5 5.4 copy.110
  76.9 5.0 fusion.69
  81.9 5.0 copy-done.1
  86.9 3.8 fusion.23
  90.7 9.3 all-gather.3.cloned.1.call-done
  100.0 5.3 copy.109
  105.3 8.2 fusion.37
  113.5 4.0 copy.112
  117.5 3.5 convert_element_type.128
  127.9 6.7 gather_fusion.4
  137.1 3.6 copy.119
  140.7 5.1 all-to-all-start
  156.3 4.6 mul.269
  160.9 5.4 scatter_custom_fusion.2
  169.6 12.0 gather_fusion.8
  184.8 7.0 gather_fusion.6
  194.3 3.7 copy.124
  197.9 5.3 all-to-all-start.2
  203.3 35.2 %fusion.2 = (bf16[8,4,29,3072]{3,2,0,1:T(8,128)(2,1)S(1)}, f32[4,8,29,3072]{3,2,1,0:T(8,128)}) fusion(bf16[4,3072,768,1]{2,1,3,0:T(8,128)(2,1)} %bitcast.184, bf16[8,4,29,768]{3,1,2,0:T(4,128)(2,1)} %all-to-all-done), kind=kOutput, calls=%fused_computation.24 | convolution fusion | flops 4564156416 | bytes 37404672 | tf_op jit(solution)/shard_map/secd,efd->secf/dot_general | solution.py:184
  238.4 11.5 fusion.30
  252.1 5.6 all-to-all-start.1
  257.7 13.6 fusion.8
  271.3 11.5 fusion.31
  285.1 7.3 all-to-all-done.1
  292.4 4.3 all-to-all-start.3
  310.4 6.7 gather_fusion.5
  317.1 4.4 reshape.414
  321.5 7.5 multiply_reduce_fusion.1
  342.2 6.7 gather_fusion.7
  348.9 4.6 reshape.418
  353.5 6.0 reduce_sum.241
  359.5 5.4 fusion.41
  371.4 3.8 copy.130
  375.2 14.9 multiply_reduce_fusion
  390.2 9.9 multiply_convert_fusion
  400.1 4.2 broadcast_multiply_fusion
  404.7 7.5 copy.133
  412.3 9.9 fusion.25
  422.2 7.5 copy.135
  429.8 7.7 fusion.38
  437.5 4.0 copy.131
  441.5 3.5 reshape.420
  446.9 3.8 fusion.44
  450.8 23.9 %reduce-scatter.3.cloned.1.call-done = f32[3,144,768]{2,1,0:T(8,128)} async-done(((f32[3,576,768]{2,1,0:T(8,128)}), f32[3,144,768]{2,1,0:T(8,128)}) %reduce-scatter.3.cloned.1.call-update) | async-done | bytes 1327120 | tf_op jit(solution)/shard_map/reduce_scatter | solution.py:280
  477.0 63.2 %reduce-scatter.5.cloned.1.call-done = f32[3,144,768]{2,1,0:T(8,128)} async-done(((f32[3,576,768]{2,1,0:T(8,128)}), f32[3,144,768]{2,1,0:T(8,128)}) %reduce-scatter.5.cloned.1.call-update) | async-done | bytes 1327120 | tf_op jit(solution)/shard_map/reduce_scatter | solution.py:286
  542.4 6.5 fusion.42
  549.0 12.4 bitcast_convert_fusion
  561.3 12.1 bitcast_convert_fusion.1
  573.5 173.9 %all-reduce.16.cloned.1.call-done = (f32[768,2304]{1,0:T(8,128)}, f32[768,768]{1,0:T(8,128)}, f32[768,32]{0,1:T(8,128)}) async-done(((f32[768,2304]{1,0:T(8,128)}, f32[768,768]{1,0:T(8,128)}, f32[768,32]{0,1:T(8,128)}), (f32[768,2304]{1,0:T(8,128)}, f32[768,768]{1,0:T(8,128)}, f32[768,32]{0,1:T(8,128)})) %all-reduce.16.cloned.1.call-update) | async-done | bytes 9535504 | tf_op jit(solution)/shard_map/psum | solution.py:314
  750.6 5.5 multiply_reduce_fusion.4
  756.1 28.9 %all-reduce.7 = (f32[768]{0:T(1024)}, f32[768]{0:T(1024)}, f32[768]{0:T(1024)}, f32[768]{0:T(1024)}, f32[4]{0:T(128)}) all-reduce(f32[768]{0:T(1024)} %get-tuple-element.17, f32[768]{0:T(1024)} %get-tuple-element.26, f32[768]{0:T(1024)S(1)} %copy-done.36, f32[768]{0:T(1024)S(1)} %copy-done.37, ...), channel_id=1, replica_groups=mesh['seq'=4,'ep'=8] {'ep'}, use_global_device_ids=true, to_apply=%region_27.28 | all-reduce | flops 3076 | bytes 24608 | tf_op jit(solution)/shard_map/psum | solution.py:314
  785.0 18.3 %all-reduce.9 = (f32[768]{0:T(1024)}, f32[768]{0:T(1024)}, f32[768]{0:T(1024)}, f32[768]{0:T(1024)}, f32[4]{0:T(128)S(1)}) all-reduce(f32[768]{0:T(1024)} %get-tuple-element.28, f32[768]{0:T(1024)} %get-tuple-element.29, f32[768]{0:T(1024)} %get-tuple-element.30, ...), channel_id=1, replica_groups=mesh['seq'=4,'ep'=8] {'seq'}, use_global_device_ids=true, to_apply=%region_28.29 | all-reduce | flops 3076 | bytes 24608 | tf_op jit(solution)/shard_map/psum | solution.py:314
  809.7 591.4 %all-reduce.20.cloned.1.call-done = (bf16[12288,768]{1,0:T(8,128)(2,1)}, bf16[12288,768]{1,0:T(8,128)(2,1)}) async-done(((bf16[12288,768]{1,0:T(8,128)(2,1)}, bf16[12288,768]{1,0:T(8,128)(2,1)}), (bf16[12288,768]{1,0:T(8,128)(2,1)}, bf16[12288,768]{1,0:T(8,128)(2,1)})) %all-reduce.20.cloned.1.call-update) | async-done | bytes 37748752 | tf_op jit(solution)/shard_map/psum | solution.py:330
  1401.1 21.0 %convert_element_type.149 = f32[12288,768]{1,0:T(8,128)} convert(bf16[12288,768]{1,0:T(8,128)(2,1)} %get-tuple-element.44) | non-fusion elementwise | flops 9437184 | bytes 56623104 | tf_op jit(solution)/shard_map/convert_element_type | solution.py:330
  1422.1 4.8 copy-done.6
  1427.0 13.0 convert_element_type.152
  1440.0 158.8 %all-reduce.18.cloned.1.call-done = (f32[768,2304]{1,0:T(8,128)}, f32[768,768]{1,0:T(8,128)}, f32[768,32]{0,1:T(8,128)}) async-done(((f32[768,2304]{1,0:T(8,128)}, f32[768,768]{1,0:T(8,128)}, f32[768,32]{0,1:T(8,128)}), (f32[768,2304]{1,0:T(8,128)}, f32[768,768]{1,0:T(8,128)}, f32[768,32]{0,1:T(8,128)})) %all-reduce.18.cloned.1.call-update) | async-done | bytes 9535504 | tf_op jit(solution)/shard_map/psum | solution.py:314
  1598.8 6.6 copy.165
  (209 shorter events, 115.7 us)
Async XLA Ops:
  7.2 4.6 copy-start
  7.2 64.3 %all-gather.5.cloned.1.call-start = ((), (), s32[]{:S(2)}) async-start(), calls=%async_computation.7 | async-start | bytes 3317760 | tf_op jit(solution)/shard_map/all_gather | solution.py:151
  10.2 3.3 copy-start.32
  10.3 3.2 copy-start.34
  11.8 1.8 copy-start.12
  14.9 85.1 %all-gather.3.cloned.1.call-start = ((), (), s32[]{:S(2)}) async-start(), calls=%async_computation.6 | async-start | bytes 3317760 | tf_op jit(solution)/shard_map/all_gather | solution.py:152
  14.9 9.0 copy-start.31
  15.6 9.1 copy-start.44
  24.8 0.6 copy-start.41
  49.0 6.3 copy-start.43
  65.3 5.5 copy-start.39
  81.9 5.0 copy-start.1
  81.9 5.0 copy-start.17
  121.0 4.6 copy-start.23
  121.0 4.6 copy-start.42
  124.5 1.1 copy-start.3
  124.5 1.4 copy-start.19
  125.6 0.6 copy-start.27
  126.2 0.9 copy-start.8
  140.7 57.2 %all-to-all-start = ((bf16[8,4,29,768]{3,1,2,0:T(4,128)(2,1)}), bf16[8,4,29,768]{3,1,2,0:T(4,128)(2,1)}, u32[]{:S(2)}, u32[]{:S(2)}) async-start(bf16[8,4,29,768]{3,1,2,0:T(4,128)(2,1)} %copy.119), calls=%async_computation | async-start | bytes 2850816 | tf_op jit(solution)/shard_map/all_to_all | solution.py:126
  146.5 9.8 copy-start.25
  152.8 1.1 copy-start.7
  167.8 0.6 copy-start.15
  167.8 0.6 copy-start.21
  168.4 0.6 copy-start.29
  169.6 12.0 copy-start.38
  197.9 54.2 %all-to-all-start.2 = ((bf16[8,4,29,768]{3,1,2,0:T(4,128)(2,1)}), bf16[8,4,29,768]{3,1,2,0:T(4,128)(2,1)}, u32[]{:S(2)}, u32[]{:S(2)}) async-start(bf16[8,4,29,768]{3,1,2,0:T(4,128)(2,1)} %copy.124), calls=%async_computation.2 | async-start | bytes 2850816 | tf_op jit(solution)/shard_map/all_to_all | solution.py:126
  238.4 11.5 copy-start.46
  252.1 40.3 %all-to-all-start.1 = ((bf16[8,4,29,768]{3,1,2,0:T(4,128)(2,1)}), bf16[8,4,29,768]{3,1,2,0:T(4,128)(2,1)}, u32[]{:S(2)}, u32[]{:S(2)}) async-start(bf16[8,4,29,768]{3,1,2,0:T(4,128)(2,1)} %copy.121), calls=%async_computation.1 | async-start | bytes 2850816 | tf_op jit(solution)/shard_map/all_to_all | solution.py:129
  271.3 11.5 copy-start.45
  282.8 15.0 copy-start.40
  292.4 41.3 %all-to-all-start.3 = ((bf16[8,4,29,768]{3,1,2,0:T(4,128)(2,1)}), bf16[8,4,29,768]{3,1,2,0:T(4,128)(2,1)}, u32[]{:S(2)}, u32[]{:S(2)}) async-start(bf16[8,4,29,768]{3,1,2,0:T(4,128)(2,1)} %copy.126), calls=%async_computation.3 | async-start | bytes 2850816 | tf_op jit(solution)/shard_map/all_to_all | solution.py:129
  296.7 178.0 %reduce-scatter.3.cloned.1.call-start = ((), (), s32[]{:S(2)}) async-start(), calls=%async_computation.8 | async-start | bytes 6635520 | tf_op jit(solution)/shard_map/reduce_scatter | solution.py:280
  321.5 9.8 copy-start.22
  321.5 9.8 copy-start.30
  353.5 6.0 copy-start.20
  353.5 6.0 copy-start.24
  353.5 6.0 copy-start.26
  353.5 6.0 copy-start.28
  359.5 5.5 copy-start.4
  359.5 5.4 copy-start.11
  364.9 1.7 copy-start.10
  365.5 1.1 copy-start.5
  375.2 14.9 copy-start.16
  390.2 9.9 copy-start.9
  400.1 4.6 copy-start.2
  412.2 127.9 %reduce-scatter.5.cloned.1.call-start = ((), (), s32[]{:S(2)}) async-start(), calls=%async_computation.9 | async-start | bytes 6635520 | tf_op jit(solution)/shard_map/reduce_scatter | solution.py:286
  429.7 317.7 %all-reduce.16.cloned.1.call-start = ((), (), s32[]{:S(2)}) async-start(), calls=%async_computation.10 | async-start | bytes 19070976 | tf_op jit(solution)/shard_map/psum | solution.py:314
  541.5 0.8 copy-start.13
  548.9 852.2 %all-reduce.20.cloned.1.call-start = ((), (), s32[]{:S(2)}) async-start(), calls=%async_computation.12 | async-start | bytes 75497472 | tf_op jit(solution)/shard_map/psum | solution.py:330
  573.5 1025.3 %all-reduce.18.cloned.1.call-start = ((), (), s32[]{:S(2)}) async-start(), calls=%async_computation.11 | async-start | bytes 19070976 | tf_op jit(solution)/shard_map/psum | solution.py:314
  747.4 3.2 copy-start.33
  747.4 3.2 copy-start.35
  750.6 5.5 copy-start.36
  750.6 5.5 copy-start.37
  1401.1 25.9 %copy-start.6 = (bf16[12288,768]{1,0:T(8,128)(2,1)S(1)}, bf16[12288,768]{1,0:T(8,128)(2,1)}, u32[]{:S(2)}) copy-start(bf16[12288,768]{1,0:T(8,128)(2,1)} %get-tuple-element.45) | copy-start | bytes 56623108
  1598.8 6.6 copy-start.14
  1605.4 1.4 copy-start.18
Sparse Core Ops, SparseCore 0:
  15.0 42.6 all-gather.4
  60.1 39.9 all-gather.2
  412.3 62.3 reduce-scatter.2
  478.1 61.9 reduce-scatter.4
  549.0 198.3 all-reduce.15
  752.1 648.9 all-reduce.19
  1405.0 193.7 all-reduce.17
